TPU v7x, 128 devices: a whole 4x4x4 slice. The times are simulated.
128 devices in a mesh: pipe: 4 (over y), tensor: 32 (over z, x, core).
Axes of the slice: x: 4, y: 4, z: 4, core: 2. Of those that a mesh axis runs over, the one named last changes fastest.
Arguments:
- inputs: bfloat16 [8, 128, 8192], P(None, None, 'tensor'), may hold values from -60 to 60
- cotangent: bfloat16 [8, 128, 8192], P(None, None, 'tensor'), may hold values from -13 to 13
- norm_gain: float32 [4, 8192], P('pipe', 'tensor'), may hold values from 0.25 to 1.75
- first_factor: bfloat16 [4, 64, 128, 512], P('pipe', 'tensor'), may hold values from -0.35355339 to 0.35355339
- second_factor: bfloat16 [4, 128, 256, 256], P('pipe', 'tensor'), may hold values from -0.25 to 0.25
- third_factor: bfloat16 [4, 128, 256, 256], P('pipe', 'tensor'), may hold values from -0.3125 to 0.3125
- fourth_factor: bfloat16 [4, 64, 512, 128], P('pipe', 'tensor'), may hold values from -0.22097087 to 0.22097087
Outputs:
- section_out: bfloat16 [4, 8, 128, 8192], P('pipe', None, None, 'tensor')
- section_grad: bfloat16 [4, 8, 128, 8192], P('pipe', None, None, 'tensor')
- gain_grad: float32 [4, 8192], P('pipe', 'tensor')
- first_grad: float32 [4, 64, 128, 512], P('pipe', 'tensor')
- second_grad: float32 [4, 128, 256, 256], P('pipe', 'tensor')
- third_grad: float32 [4, 128, 256, 256], P('pipe', 'tensor')
- fourth_grad: float32 [4, 64, 512, 128], P('pipe', 'tensor')
All inputs are finite; a program needn't handle non-finite values.
Results may differ from a plain program's by a relative error of at most 0.013.
Values may be sent and summed in bfloat16 or wider, within the bound.
No kernel may reach another device: no remote copies, remote signals or barrier semaphores. Data moves between devices by JAX's collectives and lax.ppermute only.
A program may use at most 128 MiB of HBM per device.

v0:
```python
import math
import jax
import jax.numpy as jnp
from jax import lax
from jax.sharding import PartitionSpec as P

EPS = 1e-05
TANH_SCALE = math.sqrt(2.0 / math.pi)
CUBIC_COEF = 0.044715


def from_behind(array, axis, by):
    size = lax.axis_size(axis)
    pairs = [(i, i + by) for i in range(size) if 0 <= i + by < size]
    return lax.ppermute(array, axis, pairs)


def gelu_pair(preact):
    tanh_val = jnp.tanh(TANH_SCALE * (preact + CUBIC_COEF * preact * preact * preact))
    gelu_value = 0.5 * preact * (1.0 + tanh_val)
    gelu_slope = 0.5 * (1.0 + tanh_val) + 0.5 * preact * (
        1.0 - tanh_val * tanh_val
    ) * TANH_SCALE * (1.0 + 3.0 * CUBIC_COEF * preact * preact)
    return (gelu_value, gelu_slope)


def row_total(values):
    return lax.psum(values, "tensor")


def to_hidden(values):
    return lax.all_to_all(values, "tensor", split_axis=3, concat_axis=1, tiled=True)


def to_features(values):
    return lax.all_to_all(values, "tensor", split_axis=1, concat_axis=3, tiled=True)


def load_at(stored, micro_slot):
    return lax.dynamic_index_in_dim(stored, micro_slot, 0, keepdims=False)


def store_at(stored, member, micro_slot, is_valid):
    former = lax.dynamic_index_in_dim(stored, micro_slot, 0, keepdims=False)
    return lax.dynamic_update_index_in_dim(
        stored, jnp.where(is_valid, member, former), micro_slot, 0
    )


def body(inputs, cotangent, norm_gain, first_factor, second_factor, third_factor, fourth_factor):
    sections = lax.axis_size("pipe")
    section_id = lax.axis_index("pipe")
    micro_count, tokens, width_dev = inputs.shape
    full_width = width_dev * lax.axis_size("tensor")
    blocks = first_factor.shape[1]
    block_size = first_factor.shape[2]
    expand = first_factor.shape[3] // block_size
    col_blocks = second_factor.shape[1]
    mix_width = second_factor.shape[2]
    all_blocks = mix_width // expand
    gain_row = norm_gain[0]
    factor_one = first_factor[0].reshape(blocks, block_size, expand, block_size)
    factor_two = second_factor[0].reshape(col_blocks, all_blocks, expand, mix_width)
    factor_three = third_factor[0].reshape(col_blocks, mix_width, all_blocks, expand)
    factor_four = fourth_factor[0].reshape(blocks, expand, block_size, block_size)
    ticks = micro_count + sections - 1
    carry = jnp.zeros((tokens, width_dev), jnp.bfloat16)
    out_buffer = jnp.zeros((micro_count, tokens, width_dev), jnp.bfloat16)
    records = None
    for tick_now in range(ticks):
        micro_id = tick_now - section_id
        is_valid = (micro_id >= 0) & (micro_id < micro_count)
        micro_slot = jnp.clip(micro_id, 0, micro_count - 1)
        stream_in = jnp.where(section_id == 0, load_at(inputs, micro_slot), carry)
        forward_stream = stream_in.astype(jnp.float32)
        sum_sq = row_total(jnp.sum(forward_stream * forward_stream, axis=-1))
        forward_inv_rms = lax.rsqrt(sum_sq / full_width + EPS)
        forward_normed = (forward_stream * forward_inv_rms[:, None] * gain_row).astype(jnp.bfloat16)
        spread = jnp.einsum(
            "tij,ijak->tiak",
            forward_normed.reshape(tokens, blocks, block_size),
            factor_one,
            preferred_element_type=jnp.float32,
        ).astype(jnp.bfloat16)
        forward_hidden_in = to_hidden(spread)
        activations_preact = jnp.einsum(
            "tiac,ciae->tce", forward_hidden_in, factor_two, preferred_element_type=jnp.float32
        )
        activations_gelu_value, activations_gelu_slope = gelu_pair(activations_preact)
        middle_activated = activations_gelu_value.astype(jnp.bfloat16)
        mixed_out = jnp.einsum(
            "tce,ceia->tiac", middle_activated, factor_three, preferred_element_type=jnp.float32
        ).astype(jnp.bfloat16)
        forward_feature_in = to_features(mixed_out)
        branch = jnp.einsum(
            "tiak,iakj->tij", forward_feature_in, factor_four, preferred_element_type=jnp.float32
        )
        forward_branch = branch.reshape(forward_feature_in.shape[0], width_dev)
        result = (forward_stream + forward_branch).astype(jnp.bfloat16)
        forward_record = (
            stream_in,
            forward_inv_rms,
            forward_hidden_in,
            forward_feature_in,
            activations_preact,
            middle_activated,
        )
        result, record = (result, forward_record)
        out_buffer = store_at(out_buffer, result, micro_slot, is_valid)
        if records is None:
            records = [jnp.zeros((micro_count,) + member.shape, member.dtype) for member in record]
        records = [
            store_at(stored, member, micro_slot, is_valid)
            for stored, member in zip(records, record)
        ]
        if tick_now + 1 < ticks:
            carry = from_behind(result, "pipe", 1)
    grad_carry = jnp.zeros((tokens, width_dev), jnp.bfloat16)
    grad_buffer = jnp.zeros((micro_count, tokens, width_dev), jnp.bfloat16)
    running = [
        jnp.zeros((width_dev,), jnp.float32),
        jnp.zeros((blocks, block_size, expand, block_size), jnp.float32),
        jnp.zeros((col_blocks, all_blocks, expand, mix_width), jnp.float32),
        jnp.zeros((col_blocks, mix_width, all_blocks, expand), jnp.float32),
        jnp.zeros((blocks, expand, block_size, block_size), jnp.float32),
    ]
    for tick_now in range(ticks):
        micro_id = tick_now - (sections - 1 - section_id)
        is_valid = (micro_id >= 0) & (micro_id < micro_count)
        micro_slot = jnp.clip(micro_id, 0, micro_count - 1)
        grad_out = jnp.where(section_id == sections - 1, load_at(cotangent, micro_slot), grad_carry)
        record = tuple((load_at(stored, micro_slot) for stored in records))
        backward_stream_in, inv_rms, hidden_in, feature_in, preact, activated = record
        stream = backward_stream_in.astype(jnp.float32)
        inv_col = inv_rms[:, None]
        grad_blocks = grad_out.reshape(tokens, blocks, block_size)
        backward_part_four = jnp.einsum(
            "tiak,tij->iakj", feature_in, grad_blocks, preferred_element_type=jnp.float32
        )
        grad_feat = jnp.einsum(
            "tij,iakj->tiak", grad_blocks, factor_four, preferred_element_type=jnp.float32
        ).astype(jnp.bfloat16)
        grad_hidden = to_hidden(grad_feat)
        backward_part_three = jnp.einsum(
            "tce,tiac->ceia", activated, grad_hidden, preferred_element_type=jnp.float32
        )
        grad_act = jnp.einsum(
            "tiac,ceia->tce", grad_hidden, factor_three, preferred_element_type=jnp.float32
        )
        gelu_value, gelu_slope = gelu_pair(preact)
        grad_pre = (grad_act * gelu_slope).astype(jnp.bfloat16)
        backward_part_two = jnp.einsum(
            "tiac,tce->ciae", hidden_in, grad_pre, preferred_element_type=jnp.float32
        )
        grad_mix = jnp.einsum(
            "tce,ciae->tiac", grad_pre, factor_two, preferred_element_type=jnp.float32
        ).astype(jnp.bfloat16)
        grad_spread = to_features(grad_mix)
        normed = (
            (stream * inv_col * gain_row).astype(jnp.bfloat16).reshape(tokens, blocks, block_size)
        )
        backward_part_one = jnp.einsum(
            "tij,tiak->ijak", normed, grad_spread, preferred_element_type=jnp.float32
        )
        grad_norm = jnp.einsum(
            "tiak,ijak->tij", grad_spread, factor_one, preferred_element_type=jnp.float32
        ).reshape(tokens, width_dev)
        backward_part_gain = jnp.sum(grad_norm * stream * inv_col, axis=0)
        scaled_grad = grad_norm * gain_row
        inner_sum = row_total(jnp.sum(scaled_grad * stream, axis=-1))[:, None]
        grad_in = (
            grad_out.astype(jnp.float32)
            + scaled_grad * inv_col
            - stream * inv_col * inv_col * inv_col * inner_sum / full_width
        ).astype(jnp.bfloat16)
        grad_in, parts = (
            grad_in,
            (
                backward_part_gain,
                backward_part_one,
                backward_part_two,
                backward_part_three,
                backward_part_four,
            ),
        )
        running = [
            total + jnp.where(is_valid, member, 0.0) for total, member in zip(running, parts)
        ]
        grad_buffer = store_at(grad_buffer, grad_in, micro_slot, is_valid)
        if tick_now + 1 < ticks:
            grad_carry = from_behind(grad_in, "pipe", -1)
    part_gain, part_one, part_two, part_three, part_four = running
    return (
        out_buffer[None],
        grad_buffer[None],
        part_gain[None],
        part_one.reshape(1, blocks, block_size, expand * block_size),
        part_two.reshape(1, col_blocks, mix_width, mix_width),
        part_three.reshape(1, col_blocks, mix_width, mix_width),
        part_four.reshape(1, blocks, expand * block_size, block_size),
    )


def solution(mesh):
    placed = (
        P(None, None, "tensor"),
        P(None, None, "tensor"),
        P("pipe", "tensor"),
        P("pipe", "tensor", None, None),
        P("pipe", "tensor", None, None),
        P("pipe", "tensor", None, None),
        P("pipe", "tensor", None, None),
    )
    return jax.shard_map(
        body,
        mesh=mesh,
        in_specs=placed,
        out_specs=(
            P("pipe", None, None, "tensor"),
            P("pipe", None, None, "tensor"),
            P("pipe", "tensor"),
            P("pipe", "tensor", None, None),
            P("pipe", "tensor", None, None),
            P("pipe", "tensor", None, None),
            P("pipe", "tensor", None, None),
        ),
        check_vma=False,
    )
```

profile of v0, /device:TPU:24, one launch (start us, length us, event | category | flops | bytes accessed | tf_op | source)
XLA Modules:
  0.0 2443.7 jit_solution(7076076025298770680)
XLA Ops:
  3.2 68.3 %psum.154 = f32[128]{0:T(128)S(1)} all-reduce(f32[128]{0:T(128)S(1)} %fusion.491), channel_id=1, replica_groups=mesh['pipe'=4,'tensor'=32] {'tensor'}, use_global_device_ids=true, to_apply=%region_1.2 | all-reduce | flops 128 | bytes 1024 | tf_op jit(solution)/shard_map/psum | solution.py:28
  95.8 7.4 all-to-all-start.22
  132.4 64.3 %psum.155 = f32[128]{0:T(128)S(1)} all-reduce(f32[128]{0:T(128)S(1)} %fusion.321), channel_id=1, replica_groups=mesh['pipe'=4,'tensor'=32] {'tensor'}, use_global_device_ids=true, to_apply=%region_3.4 | all-reduce | flops 128 | bytes 1024 | tf_op jit(solution)/shard_map/psum | solution.py:28
  242.2 63.8 %psum.156 = f32[128]{0:T(128)S(1)} all-reduce(f32[128]{0:T(128)S(1)} %fusion.325), channel_id=1, replica_groups=mesh['pipe'=4,'tensor'=32] {'tensor'}, use_global_device_ids=true, to_apply=%region_5.6 | all-reduce | flops 128 | bytes 1024 | tf_op jit(solution)/shard_map/psum | solution.py:28
  352.9 63.9 %psum.157 = f32[128]{0:T(128)S(1)} all-reduce(f32[128]{0:T(128)S(1)} %fusion.329), channel_id=1, replica_groups=mesh['pipe'=4,'tensor'=32] {'tensor'}, use_global_device_ids=true, to_apply=%region_7.8 | all-reduce | flops 128 | bytes 1024 | tf_op jit(solution)/shard_map/psum | solution.py:28
  463.6 63.9 %psum.158 = f32[128]{0:T(128)S(1)} all-reduce(f32[128]{0:T(128)S(1)} %fusion.333), channel_id=1, replica_groups=mesh['pipe'=4,'tensor'=32] {'tensor'}, use_global_device_ids=true, to_apply=%region_9.10 | all-reduce | flops 128 | bytes 1024 | tf_op jit(solution)/shard_map/psum | solution.py:28
  574.7 63.9 %psum.159 = f32[128]{0:T(128)S(1)} all-reduce(f32[128]{0:T(128)S(1)} %fusion.337), channel_id=1, replica_groups=mesh['pipe'=4,'tensor'=32] {'tensor'}, use_global_device_ids=true, to_apply=%region_11.12 | all-reduce | flops 128 | bytes 1024 | tf_op jit(solution)/shard_map/psum | solution.py:28
  685.4 63.9 %psum.160 = f32[128]{0:T(128)S(1)} all-reduce(f32[128]{0:T(128)S(1)} %fusion.341), channel_id=1, replica_groups=mesh['pipe'=4,'tensor'=32] {'tensor'}, use_global_device_ids=true, to_apply=%region_13.14 | all-reduce | flops 128 | bytes 1024 | tf_op jit(solution)/shard_map/psum | solution.py:28
  796.1 63.9 %psum.161 = f32[128]{0:T(128)S(1)} all-reduce(f32[128]{0:T(128)S(1)} %fusion.345), channel_id=1, replica_groups=mesh['pipe'=4,'tensor'=32] {'tensor'}, use_global_device_ids=true, to_apply=%region_15.16 | all-reduce | flops 128 | bytes 1024 | tf_op jit(solution)/shard_map/psum | solution.py:28
  907.0 63.9 %psum.162 = f32[128]{0:T(128)S(1)} all-reduce(f32[128]{0:T(128)S(1)} %fusion.349), channel_id=1, replica_groups=mesh['pipe'=4,'tensor'=32] {'tensor'}, use_global_device_ids=true, to_apply=%region_17.18 | all-reduce | flops 128 | bytes 1024 | tf_op jit(solution)/shard_map/psum | solution.py:28
  1017.7 63.9 %psum.163 = f32[128]{0:T(128)S(1)} all-reduce(f32[128]{0:T(128)S(1)} %fusion.353), channel_id=1, replica_groups=mesh['pipe'=4,'tensor'=32] {'tensor'}, use_global_device_ids=true, to_apply=%region_19.20 | all-reduce | flops 128 | bytes 1024 | tf_op jit(solution)/shard_map/psum | solution.py:28
  1128.4 63.9 %psum.164 = f32[128]{0:T(128)S(1)} all-reduce(f32[128]{0:T(128)S(1)} %fusion.357), channel_id=1, replica_groups=mesh['pipe'=4,'tensor'=32] {'tensor'}, use_global_device_ids=true, to_apply=%region_21.22 | all-reduce | flops 128 | bytes 1024 | tf_op jit(solution)/shard_map/psum | solution.py:28
  1229.5 7.5 all-to-all-start.23
  1249.9 64.6 %psum.165 = f32[128]{0:T(128)S(1)} all-reduce(f32[128]{0:T(128)} %get-tuple-element.29), channel_id=1, replica_groups=mesh['pipe'=4,'tensor'=32] {'tensor'}, use_global_device_ids=true, to_apply=%region_23.24 | all-reduce | flops 128 | bytes 1024 | tf_op jit(solution)/shard_map/psum | solution.py:28
  1362.6 65.1 %psum.166 = f32[128]{0:T(128)} all-reduce(f32[128]{0:T(128)} %get-tuple-element.31), channel_id=1, replica_groups=mesh['pipe'=4,'tensor'=32] {'tensor'}, use_global_device_ids=true, to_apply=%region_25.26 | all-reduce | flops 128 | bytes 1024 | tf_op jit(solution)/shard_map/psum | solution.py:28
  1472.8 65.1 %psum.167 = f32[128]{0:T(128)} all-reduce(f32[128]{0:T(128)} %get-tuple-element.33), channel_id=1, replica_groups=mesh['pipe'=4,'tensor'=32] {'tensor'}, use_global_device_ids=true, to_apply=%region_27.28 | all-reduce | flops 128 | bytes 1024 | tf_op jit(solution)/shard_map/psum | solution.py:28
  1584.4 65.1 %psum.168 = f32[128]{0:T(128)} all-reduce(f32[128]{0:T(128)} %get-tuple-element.35), channel_id=1, replica_groups=mesh['pipe'=4,'tensor'=32] {'tensor'}, use_global_device_ids=true, to_apply=%region_29.30 | all-reduce | flops 128 | bytes 1024 | tf_op jit(solution)/shard_map/psum | solution.py:28
  1696.1 65.1 %psum.169 = f32[128]{0:T(128)} all-reduce(f32[128]{0:T(128)} %get-tuple-element.37), channel_id=1, replica_groups=mesh['pipe'=4,'tensor'=32] {'tensor'}, use_global_device_ids=true, to_apply=%region_31.32 | all-reduce | flops 128 | bytes 1024 | tf_op jit(solution)/shard_map/psum | solution.py:28
  1807.9 65.1 %psum.170 = f32[128]{0:T(128)} all-reduce(f32[128]{0:T(128)} %get-tuple-element.39), channel_id=1, replica_groups=mesh['pipe'=4,'tensor'=32] {'tensor'}, use_global_device_ids=true, to_apply=%region_33.34 | all-reduce | flops 128 | bytes 1024 | tf_op jit(solution)/shard_map/psum | solution.py:28
  1919.5 65.1 %psum.171 = f32[128]{0:T(128)} all-reduce(f32[128]{0:T(128)} %get-tuple-element.41), channel_id=1, replica_groups=mesh['pipe'=4,'tensor'=32] {'tensor'}, use_global_device_ids=true, to_apply=%region_35.36 | all-reduce | flops 128 | bytes 1024 | tf_op jit(solution)/shard_map/psum | solution.py:28
  2031.1 65.1 %psum.172 = f32[128]{0:T(128)} all-reduce(f32[128]{0:T(128)} %get-tuple-element.43), channel_id=1, replica_groups=mesh['pipe'=4,'tensor'=32] {'tensor'}, use_global_device_ids=true, to_apply=%region_37.38 | all-reduce | flops 128 | bytes 1024 | tf_op jit(solution)/shard_map/psum | solution.py:28
  2142.9 65.1 %psum.173 = f32[128]{0:T(128)} all-reduce(f32[128]{0:T(128)} %get-tuple-element.45), channel_id=1, replica_groups=mesh['pipe'=4,'tensor'=32] {'tensor'}, use_global_device_ids=true, to_apply=%region_39.40 | all-reduce | flops 128 | bytes 1024 | tf_op jit(solution)/shard_map/psum | solution.py:28
  2254.5 65.1 %psum.174 = f32[128]{0:T(128)} all-reduce(f32[128]{0:T(128)} %get-tuple-element.47), channel_id=1, replica_groups=mesh['pipe'=4,'tensor'=32] {'tensor'}, use_global_device_ids=true, to_apply=%region_41.42 | all-reduce | flops 128 | bytes 1024 | tf_op jit(solution)/shard_map/psum | solution.py:28
  2368.3 64.6 %psum.175 = f32[128]{0:T(128)S(1)} all-reduce(f32[128]{0:T(128)S(1)} %get-tuple-element.49), channel_id=1, replica_groups=mesh['pipe'=4,'tensor'=32] {'tensor'}, use_global_device_ids=true, to_apply=%region_43.44 | all-reduce | flops 128 | bytes 1024 | tf_op jit(solution)/shard_map/psum | solution.py:28
  (883 shorter events, 1002.5 us)
Async XLA Ops:
  74.3 21.6 all-to-all-start
  95.8 16.2 all-to-all-start.22
  198.0 13.4 all-to-all-start.2
  218.0 13.6 all-to-all-start.3
  550.3 13.8 all-to-all-start.9
  882.8 13.5 all-to-all-start.15
  1104.4 13.4 all-to-all-start.19
  1195.2 13.4 all-to-all-start.20
  1215.1 14.4 all-to-all-start.21
  1229.5 16.3 all-to-all-start.23
  1327.6 13.4 all-to-all-start.24
  1455.9 13.8 all-to-all-start.27
  1549.4 13.4 all-to-all-start.28
  1567.8 13.4 all-to-all-start.29
  1661.1 13.4 all-to-all-start.30
  1679.5 13.4 all-to-all-start.31
  1772.7 13.4 all-to-all-start.32
  1791.1 13.5 all-to-all-start.33
  1996.1 13.4 all-to-all-start.36
  2014.5 13.4 all-to-all-start.37
  2126.1 13.6 all-to-all-start.39
  2219.5 13.4 all-to-all-start.40
  2237.9 13.4 all-to-all-start.41
  2332.2 13.4 all-to-all-start.42
  (182 other events, 1792.8 us)
where the time goes:
time: 2460 us; the launch traced here: 2440 us
  blocking collectives  1420 us (58%)
  starting transfers between devices  258 us (10%)
  local copies, waits for them, and re-layouts  256 us (10%)
  waiting for transfers between devices  235 us (10%)
  matrix products  175 us (7%)
  other arithmetic  93.8 us (4%)
    psum x22, blocking collectives, row_total(): return lax.psum(values, 'tensor')  1420 us
    all_to_all x22, waiting for transfers between devices, to_hidden(): lax.all_to_all(values, 'tensor', split_axis=3, concat_axis=1, tiled=True)  119 us
    all_to_all x22, starting transfers between devices, to_features(): lax.all_to_all(values, 'tensor', split_axis=1, concat_axis=3, tiled=True)  105 us
    all_to_all x22, starting transfers between devices, to_hidden(): lax.all_to_all(values, 'tensor', split_axis=3, concat_axis=1, tiled=True)  103 us
    all_to_all x22, waiting for transfers between devices, to_features(): lax.all_to_all(values, 'tensor', split_axis=1, concat_axis=3, tiled=True)  82.4 us
    dynamic_update_slice x63, other arithmetic, store_at(): lax.dynamic_update_index_in_dim(stored, jnp.where(is_valid, member, forme...  76.8 us
    dynamic_slice x47, local copies, waits for them, and re-layouts, store_at(): former = lax.dynamic_index_in_dim(stored, micro_slot, 0, keepdims=False)  73.1 us
    ppermute x20, starting transfers between devices, from_behind(): return lax.ppermute(array, axis, pairs)  50.4 us
  transfers between devices with their start and end apart: 64, of which 52 were waited for; matrix products, arithmetic and copies ran while one was open for 10% of the time, Pallas kernels for 0%

commit v1 on v0

--- a/solution.py
+++ b/solution.py
@@ -25,7 +25,7 @@
 
 
 def row_total(values):
-    return lax.psum(values, "tensor")
+    return jnp.sum(lax.all_gather(values, "tensor"), axis=0)
 
 
 def to_hidden(values):

time: 2460 us -> 1510 us (0.61)
  blocking collectives: 1420 us -> 455 us
  starting transfers between devices: 258 us -> 284 us
    psum x22 -> x0, blocking collectives: 1420 us -> none  [row_total(): return lax.psum(values, 'tensor')]
    all_gather x0 -> x22, blocking collectives: none -> 455 us  [row_total(): return jnp.sum(lax.all_gather(values, 'tensor'), axis=0)]
    all_to_all x22, starting transfers between devices: 103 us -> 129 us  [to_hidden(): lax.all_to_all(values, 'tensor', split_axis=3, concat_axis=1, tiled=True)]
  transfers between devices with their start and end apart: 64 -> 64, of which waited for: 52 -> 52; matrix products, arithmetic and copies ran while one was open for 10% -> 16% of each run, Pallas kernels for 0% -> 0%
where the time goes in v1:
time: 1510 us; the launch traced here: 1490 us
  blocking collectives  455 us (30%)
  starting transfers between devices  284 us (19%)
  waiting for transfers between devices  240 us (16%)
  local copies, waits for them, and re-layouts  235 us (16%)
  matrix products  169 us (11%)
  other arithmetic  100 us (7%)
    all_gather x22, blocking collectives, row_total(): return jnp.sum(lax.all_gather(values, 'tensor'), axis=0)  455 us
    all_to_all x22, waiting for transfers between devices, to_hidden(): lax.all_to_all(values, 'tensor', split_axis=3, concat_axis=1, tiled=True)  134 us
    all_to_all x22, starting transfers between devices, to_hidden(): lax.all_to_all(values, 'tensor', split_axis=3, concat_axis=1, tiled=True)  129 us
    all_to_all x22, starting transfers between devices, to_features(): lax.all_to_all(values, 'tensor', split_axis=1, concat_axis=3, tiled=True)  104 us
    dynamic_update_slice x63, other arithmetic, store_at(): lax.dynamic_update_index_in_dim(stored, jnp.where(is_valid, member, forme...  74.9 us
    dynamic_slice x47, local copies, waits for them, and re-layouts, store_at(): former = lax.dynamic_index_in_dim(stored, micro_slot, 0, keepdims=False)  73.9 us
    all_to_all x22, waiting for transfers between devices, to_features(): lax.all_to_all(values, 'tensor', split_axis=1, concat_axis=3, tiled=True)  73.6 us
    ppermute x20, starting transfers between devices, from_behind(): return lax.ppermute(array, axis, pairs)  50.9 us
  transfers between devices with their start and end apart: 64, of which 52 were waited for; matrix products, arithmetic and copies ran while one was open for 16% of the time, Pallas kernels for 0%

profile of v1, /device:TPU:24, one launch (start us, length us, event | category | flops | bytes accessed | tf_op | source)
XLA Modules:
  0.0 1487.4 jit_solution(289564601743907986)
XLA Ops:
  3.2 22.8 %all-gather.22 = f32[32,1,128]{2,1,0:T(1,128)S(1)} all-gather(f32[1,1,128]{2,1,0:T(1,128)S(1)} %bitcast.2388), channel_id=2, replica_groups=mesh['pipe'=4,'tensor'=32] {'tensor'}, dimensions={0}, use_global_device_ids=true | all-gather | bytes 16896 | tf_op jit(solution)/shard_map/all_gather | solution.py:28
  52.7 7.4 all-to-all-start.22
  89.4 20.4 %all-gather.23 = f32[32,1,128]{2,1,0:T(1,128)S(1)} all-gather(f32[1,1,128]{2,1,0:T(1,128)S(1)} %bitcast.2389), channel_id=3, replica_groups=mesh['pipe'=4,'tensor'=32] {'tensor'}, dimensions={0}, use_global_device_ids=true | all-gather | bytes 16896 | tf_op jit(solution)/shard_map/all_gather | solution.py:28
  155.6 19.8 %all-gather.24 = f32[32,1,128]{2,1,0:T(1,128)S(1)} all-gather(f32[1,1,128]{2,1,0:T(1,128)S(1)} %bitcast.2390), channel_id=4, replica_groups=mesh['pipe'=4,'tensor'=32] {'tensor'}, dimensions={0}, use_global_device_ids=true | all-gather | bytes 16896 | tf_op jit(solution)/shard_map/all_gather | solution.py:28
  221.1 19.8 %all-gather.25 = f32[32,1,128]{2,1,0:T(1,128)S(1)} all-gather(f32[1,1,128]{2,1,0:T(1,128)S(1)} %bitcast.2391), channel_id=5, replica_groups=mesh['pipe'=4,'tensor'=32] {'tensor'}, dimensions={0}, use_global_device_ids=true | all-gather | bytes 16896 | tf_op jit(solution)/shard_map/all_gather | solution.py:28
  286.6 19.8 %all-gather.26 = f32[32,1,128]{2,1,0:T(1,128)S(1)} all-gather(f32[1,1,128]{2,1,0:T(1,128)S(1)} %bitcast.2392), channel_id=6, replica_groups=mesh['pipe'=4,'tensor'=32] {'tensor'}, dimensions={0}, use_global_device_ids=true | all-gather | bytes 16896 | tf_op jit(solution)/shard_map/all_gather | solution.py:28
  352.0 19.8 %all-gather.27 = f32[32,1,128]{2,1,0:T(1,128)S(1)} all-gather(f32[1,1,128]{2,1,0:T(1,128)S(1)} %bitcast.2393), channel_id=7, replica_groups=mesh['pipe'=4,'tensor'=32] {'tensor'}, dimensions={0}, use_global_device_ids=true | all-gather | bytes 16896 | tf_op jit(solution)/shard_map/all_gather | solution.py:28
  417.5 19.8 %all-gather.28 = f32[32,1,128]{2,1,0:T(1,128)S(1)} all-gather(f32[1,1,128]{2,1,0:T(1,128)S(1)} %bitcast.2394), channel_id=8, replica_groups=mesh['pipe'=4,'tensor'=32] {'tensor'}, dimensions={0}, use_global_device_ids=true | all-gather | bytes 16896 | tf_op jit(solution)/shard_map/all_gather | solution.py:28
  483.0 20.0 %all-gather.29 = f32[32,1,128]{2,1,0:T(1,128)S(1)} all-gather(f32[1,1,128]{2,1,0:T(1,128)S(1)} %bitcast.2395), channel_id=9, replica_groups=mesh['pipe'=4,'tensor'=32] {'tensor'}, dimensions={0}, use_global_device_ids=true | all-gather | bytes 16896 | tf_op jit(solution)/shard_map/all_gather | solution.py:28
  548.6 19.8 %all-gather.30 = f32[32,1,128]{2,1,0:T(1,128)S(1)} all-gather(f32[1,1,128]{2,1,0:T(1,128)S(1)} %bitcast.2396), channel_id=10, replica_groups=mesh['pipe'=4,'tensor'=32] {'tensor'}, dimensions={0}, use_global_device_ids=true | all-gather | bytes 16896 | tf_op jit(solution)/shard_map/all_gather | solution.py:28
  614.1 19.8 %all-gather.31 = f32[32,1,128]{2,1,0:T(1,128)S(1)} all-gather(f32[1,1,128]{2,1,0:T(1,128)S(1)} %bitcast.2397), channel_id=11, replica_groups=mesh['pipe'=4,'tensor'=32] {'tensor'}, dimensions={0}, use_global_device_ids=true | all-gather | bytes 16896 | tf_op jit(solution)/shard_map/all_gather | solution.py:28
  678.9 19.8 %all-gather.32 = f32[32,1,128]{2,1,0:T(1,128)S(1)} all-gather(f32[1,1,128]{2,1,0:T(1,128)S(1)} %bitcast.2398), channel_id=12, replica_groups=mesh['pipe'=4,'tensor'=32] {'tensor'}, dimensions={0}, use_global_device_ids=true | all-gather | bytes 16896 | tf_op jit(solution)/shard_map/all_gather | solution.py:28
  734.2 7.5 all-to-all-start.23
  754.6 21.5 %all-gather.33 = f32[32,1,128]{2,1,0:T(1,128)} all-gather(f32[1,1,128]{2,1,0:T(1,128)S(1)} %bitcast.2401), channel_id=13, replica_groups=mesh['pipe'=4,'tensor'=32] {'tensor'}, dimensions={0}, use_global_device_ids=true | all-gather | bytes 16896 | tf_op jit(solution)/shard_map/all_gather | solution.py:28
  826.1 21.5 %all-gather.34 = f32[32,1,128]{2,1,0:T(1,128)} all-gather(f32[1,1,128]{2,1,0:T(1,128)S(1)} %bitcast.2402), channel_id=14, replica_groups=mesh['pipe'=4,'tensor'=32] {'tensor'}, dimensions={0}, use_global_device_ids=true | all-gather | bytes 16896 | tf_op jit(solution)/shard_map/all_gather | solution.py:28
  894.6 21.5 %all-gather.35 = f32[32,1,128]{2,1,0:T(1,128)} all-gather(f32[1,1,128]{2,1,0:T(1,128)S(1)} %bitcast.2403), channel_id=15, replica_groups=mesh['pipe'=4,'tensor'=32] {'tensor'}, dimensions={0}, use_global_device_ids=true | all-gather | bytes 16896 | tf_op jit(solution)/shard_map/all_gather | solution.py:28
  964.9 21.5 %all-gather.36 = f32[32,1,128]{2,1,0:T(1,128)} all-gather(f32[1,1,128]{2,1,0:T(1,128)S(1)} %bitcast.2404), channel_id=16, replica_groups=mesh['pipe'=4,'tensor'=32] {'tensor'}, dimensions={0}, use_global_device_ids=true | all-gather | bytes 16896 | tf_op jit(solution)/shard_map/all_gather | solution.py:28
  1034.8 20.8 %all-gather.37 = f32[32,1,128]{2,1,0:T(1,128)} all-gather(f32[1,1,128]{2,1,0:T(1,128)S(1)} %bitcast.2405), channel_id=17, replica_groups=mesh['pipe'=4,'tensor'=32] {'tensor'}, dimensions={0}, use_global_device_ids=true | all-gather | bytes 16896 | tf_op jit(solution)/shard_map/all_gather | solution.py:28
  1105.1 21.5 %all-gather.38 = f32[32,1,128]{2,1,0:T(1,128)} all-gather(f32[1,1,128]{2,1,0:T(1,128)S(1)} %bitcast.2406), channel_id=18, replica_groups=mesh['pipe'=4,'tensor'=32] {'tensor'}, dimensions={0}, use_global_device_ids=true | all-gather | bytes 16896 | tf_op jit(solution)/shard_map/all_gather | solution.py:28
  1175.5 20.8 %all-gather.39 = f32[32,1,128]{2,1,0:T(1,128)} all-gather(f32[1,1,128]{2,1,0:T(1,128)S(1)} %bitcast.2407), channel_id=19, replica_groups=mesh['pipe'=4,'tensor'=32] {'tensor'}, dimensions={0}, use_global_device_ids=true | all-gather | bytes 16896 | tf_op jit(solution)/shard_map/all_gather | solution.py:28
  1245.3 21.5 %all-gather.40 = f32[32,1,128]{2,1,0:T(1,128)} all-gather(f32[1,1,128]{2,1,0:T(1,128)S(1)} %bitcast.2408), channel_id=20, replica_groups=mesh['pipe'=4,'tensor'=32] {'tensor'}, dimensions={0}, use_global_device_ids=true | all-gather | bytes 16896 | tf_op jit(solution)/shard_map/all_gather | solution.py:28
  1315.5 21.5 %all-gather.41 = f32[32,1,128]{2,1,0:T(1,128)} all-gather(f32[1,1,128]{2,1,0:T(1,128)S(1)} %bitcast.2409), channel_id=21, replica_groups=mesh['pipe'=4,'tensor'=32] {'tensor'}, dimensions={0}, use_global_device_ids=true | all-gather | bytes 16896 | tf_op jit(solution)/shard_map/all_gather | solution.py:28
  1385.3 21.5 %all-gather.42 = f32[32,1,128]{2,1,0:T(1,128)} all-gather(f32[1,1,128]{2,1,0:T(1,128)S(1)} %bitcast.2410), channel_id=22, replica_groups=mesh['pipe'=4,'tensor'=32] {'tensor'}, dimensions={0}, use_global_device_ids=true | all-gather | bytes 16896 | tf_op jit(solution)/shard_map/all_gather | solution.py:28
  1456.8 19.6 %all-gather.43 = f32[32,1,128]{2,1,0:T(1,128)S(1)} all-gather(f32[1,1,128]{2,1,0:T(1,128)S(1)} %bitcast.2400), channel_id=23, replica_groups=mesh['pipe'=4,'tensor'=32] {'tensor'}, dimensions={0}, use_global_device_ids=true | all-gather | bytes 16896 | tf_op jit(solution)/shard_map/all_gather | solution.py:28
  (887 shorter events, 1013.3 us)
Async XLA Ops:
  28.8 23.9 %all-to-all-start = ((bf16[128,2,4,128]{0,2,1,3:T(4,128)(2,1)}), bf16[128,2,4,128]{0,2,1,3:T(4,128)(2,1)S(1)}, u32[]{:S(2)}, u32[]{:S(2)}) async-start(bf16[128,2,4,128]{0,2,1,3:T(4,128)(2,1)} %copy.489), calls=%async_computation | async-start | bytes 524288 | tf_op jit(solution)/shard_map/all_to_all | solution.py:32
  52.7 16.2 %all-to-all-start.22 = ((bf16[128,2,4,128]{0,2,1,3:T(4,128)(2,1)}), bf16[128,2,4,128]{0,2,1,3:T(4,128)(2,1)S(1)}, u32[]{:S(2)}, u32[]{:S(2)}) async-start(bf16[128,2,4,128]{0,2,1,3:T(4,128)(2,1)} %copy.621), calls=%async_computation.22 | async-start | bytes 524288 | tf_op jit(solution)/shard_map/all_to_all | solution.py:32
  111.2 14.4 all-to-all-start.2
  176.8 14.5 all-to-all-start.4
  242.2 14.5 all-to-all-start.6
  307.7 14.5 all-to-all-start.8
  373.2 14.5 all-to-all-start.10
  438.6 14.5 all-to-all-start.12
  504.3 14.5 all-to-all-start.14
  569.7 14.5 all-to-all-start.16
  635.2 14.5 all-to-all-start.18
  700.0 14.4 all-to-all-start.20
  720.0 14.2 all-to-all-start.21
  734.2 16.3 %all-to-all-start.23 = ((bf16[128,64,4,4]{0,2,3,1:T(4,128)(2,1)}), bf16[128,64,4,4]{0,2,3,1:T(4,128)(2,1)}, u32[]{:S(2)}, u32[]{:S(2)}) async-start(bf16[128,64,4,4]{0,2,3,1:T(4,128)(2,1)} %copy.626), calls=%async_computation.23 | async-start | bytes 524288 | tf_op jit(solution)/shard_map/all_to_all | solution.py:36
  789.9 14.1 all-to-all-start.24
  858.1 14.9 all-to-all-start.26
  928.5 14.9 all-to-all-start.28
  998.9 14.3 all-to-all-start.30
  1067.9 15.6 %all-to-all-start.32 = ((bf16[128,2,4,128]{0,2,1,3:T(4,128)(2,1)}), bf16[128,2,4,128]{0,2,1,3:T(4,128)(2,1)}, u32[]{:S(2)}, u32[]{:S(2)}) async-start(bf16[128,2,4,128]{0,2,1,3:T(4,128)(2,1)} %copy.676), calls=%async_computation.32 | async-start | bytes 524288 | tf_op jit(solution)/shard_map/all_to_all | solution.py:32
  1139.1 14.9 all-to-all-start.34
  1208.8 14.9 %all-to-all-start.36 = ((bf16[128,2,4,128]{0,2,1,3:T(4,128)(2,1)}), bf16[128,2,4,128]{0,2,1,3:T(4,128)(2,1)}, u32[]{:S(2)}, u32[]{:S(2)}) async-start(bf16[128,2,4,128]{0,2,1,3:T(4,128)(2,1)} %copy.698), calls=%async_computation.36 | async-start | bytes 524288 | tf_op jit(solution)/shard_map/all_to_all | solution.py:32
  1279.0 14.9 all-to-all-start.38
  1349.4 14.1 all-to-all-start.40
  1420.2 13.9 all-to-all-start.42
  (168 other events, 1243.1 us)
